TPU v7x, 32 devices: a whole 2x2x4 slice. The times are simulated.
32 devices in a mesh: rows: 4 (over z), pos: 8 (over y, x, core).
Axes of the slice: x: 2, y: 2, z: 4, core: 2. Of those that a mesh axis runs over, the one named last changes fastest.
Arguments:
- tokens: bfloat16 [16, 2048, 768], P('rows', 'pos'), may hold values from -6 to 6
- segment_ids: int32 [16, 2048], P('rows', 'pos'), may hold values from 0 to 2, as said below
- group_sizes: int32 [16, 2], P('rows'), may hold values from 4 to 16, as said below
- prefix_lens: int32 [16, 2], P('rows'), may hold values from 1 to 768, as said below
- solution_lens: int32 [16, 2, 16], P('rows'), may hold values from 0 to 657, as said below
- padding_counts: int32 [16], P('rows'), may hold values from 0 to 128, as said below
- attn_gain: bfloat16 [768], replicated, may hold values from 0.5 to 1.5
- attn_shift: bfloat16 [768], replicated, may hold values from -1 to 1
- w_qkv: bfloat16 [768, 2304], replicated, may hold values from -0.21875 to 0.21875
- query_bias: bfloat16 [768], replicated, may hold values from -2.5 to 2.5
- value_bias: bfloat16 [768], replicated, may hold values from -1.5 to 1.5
- w_out: bfloat16 [768, 768], replicated, may hold values from -0.875 to 0.875
- out_bias: bfloat16 [768], replicated, may hold values from -1.5 to 1.5
- ffn_gain: bfloat16 [768], replicated, may hold values from 0.5 to 1.5
- ffn_shift: bfloat16 [768], replicated, may hold values from -1 to 1
- w_up: bfloat16 [768, 3072], replicated, may hold values from -0.21875 to 0.21875
- up_bias: bfloat16 [3072], replicated, may hold values from -2.5 to 2.5
- w_down: bfloat16 [3072, 768], replicated, may hold values from -0.109375 to 0.109375
- down_bias: bfloat16 [768], replicated, may hold values from -1.5 to 1.5
- cotangent: bfloat16 [16, 2048, 768], P('rows', 'pos'), may hold values from -6 to 6
Outputs:
- layer_out: bfloat16 [16, 2048, 768], P('rows', 'pos')
- tokens_grad: bfloat16 [16, 2048, 768], P('rows', 'pos')
- grad_attn_gain: float32 [768], replicated
- grad_attn_shift: float32 [768], replicated
- grad_w_qkv: float32 [768, 2304], replicated
- grad_query_bias: float32 [768], replicated
- grad_value_bias: float32 [768], replicated
- grad_w_out: float32 [768, 768], replicated
- grad_out_bias: float32 [768], replicated
- grad_ffn_gain: float32 [768], replicated
- grad_ffn_shift: float32 [768], replicated
- grad_w_up: float32 [768, 3072], replicated
- grad_up_bias: float32 [3072], replicated
- grad_w_down: float32 [3072, 768], replicated
- grad_down_bias: float32 [768], replicated
Inputs may be any that keep to these rules, and one draw needn't show every extreme that they name: `group_sizes`: each group holds this many solutions. `solution_lens`: A group's solutions at index group_sizes or more have length 0, the others 1 or more. `prefix_lens`: each prefix has 1 or more positions. `segment_ids`: A row holds group 0 (its prefix, then its solutions in order), then group 1, then padding_counts padding positions marked 2; together exactly 2048 positions. `padding_counts`: the row's positions after both groups.
All inputs are finite; a program needn't handle non-finite values.
Results may differ from a plain program's by a relative error of at most 0.012.
Values may be sent and summed in bfloat16 or wider, within the bound.
No kernel may reach another device: no remote copies, remote signals or barrier semaphores. Data moves between devices by JAX's collectives and lax.ppermute only.
A program may use at most 448 MiB of HBM per device.

v0:
```python
import math
import jax
import jax.numpy as jnp
from jax import lax
from jax.sharding import PartitionSpec as P

HEAD_DIM = 64
EPS = 1e-05
NEG = -1e30
GELU_C = 0.7978845608028654


def layer_norm(values, gain, shift):
    center = values - jnp.mean(values, axis=-1, keepdims=True)
    spread = jnp.mean(center * center, axis=-1, keepdims=True)
    return center * lax.rsqrt(spread + EPS) * gain + shift


def gelu_tanh(values):
    return 0.5 * values * (1.0 + jnp.tanh(GELU_C * (values + 0.044715 * values * values * values)))


def classes(places, segments, sizes_row, prefix_row, lens_row, padding_row, length):
    slots = jnp.arange(lens_row.shape[-1], dtype=jnp.int32)
    kept_lens = jnp.where(slots[None, None, :] < sizes_row[:, :, None], lens_row, 0)
    solution_ends = jnp.cumsum(kept_lens, axis=-1)
    totals = prefix_row + solution_ends[:, :, -1]
    starts = jnp.cumsum(totals, axis=-1) - totals
    groups = jnp.arange(sizes_row.shape[-1], dtype=jnp.int32)
    member = segments[:, :, None] == groups[None, None, :]
    group_start = jnp.sum(jnp.where(member, starts[:, None, :], 0), axis=-1)
    prefix_here = jnp.sum(jnp.where(member, prefix_row[:, None, :], 0), axis=-1)
    inside = places[None, :] - group_start - prefix_here
    passed = jnp.where(
        member[:, :, :, None], inside[:, :, None, None] >= solution_ends[:, None, :, :], False
    )
    passed_count = jnp.sum(passed.astype(jnp.int32), axis=(2, 3))
    branch = jnp.where(inside < 0, -1, passed_count)
    padded = places[None, :] >= length - padding_row[:, None]
    class_id = jnp.where(padded, -1, segments)
    branch = jnp.where(padded, -2, branch)
    return (class_id, branch)


def visible(query_class, query_branch, query_places, key_class, key_branch, key_places):
    same = query_class[:, :, None] == key_class[:, None, :]
    causal = key_places[None, None, :] <= query_places[None, :, None]
    shared = (key_branch[:, None, :] == -1) | (key_branch[:, None, :] == query_branch[:, :, None])
    return same & causal & shared


def heads_first(values):
    return values.reshape(
        values.shape[0], values.shape[1], values.shape[2] // HEAD_DIM, HEAD_DIM
    ).transpose(2, 0, 1, 3)


def heads_last(values):
    return values.transpose(1, 2, 0, 3).reshape(
        values.shape[1], values.shape[2], values.shape[0] * values.shape[3]
    )


def head_scores(query_head, key_head, allowed, score_scale):
    product = (
        jnp.einsum("rqe,rke->rqk", query_head, key_head, preferred_element_type=jnp.float32)
        * score_scale
    )
    return jnp.where(allowed, product, NEG)


def outer_sum(left, right):
    return lax.dot_general(
        left.reshape(-1, left.shape[-1]),
        right.reshape(-1, right.shape[-1]),
        (((0,), (0,)), ((), ())),
        preferred_element_type=jnp.float32,
    )


def back_through(grad, weight):
    return jnp.einsum("rpo,io->rpi", grad, weight, preferred_element_type=jnp.float32)


def column_sum(values):
    return jnp.sum(values, axis=(0, 1), dtype=jnp.float32)


def per_device(
    tokens,
    segment_ids,
    group_sizes,
    prefix_lens,
    solution_lens,
    padding_counts,
    attn_gain,
    attn_shift,
    w_qkv,
    query_bias,
    value_bias,
    w_out,
    out_bias,
    ffn_gain,
    ffn_shift,
    w_up,
    up_bias,
    w_down,
    down_bias,
    cotangent,
):
    row_count, local_len, model_width = tokens.shape
    row_len = local_len * lax.axis_size("pos")
    score_scale = 1.0 / math.sqrt(HEAD_DIM)
    local_places = lax.axis_index("pos") * local_len + jnp.arange(local_len, dtype=jnp.int32)
    all_places = jnp.arange(row_len, dtype=jnp.int32)
    inputs = tokens.astype(jnp.float32)
    normed_one, norm_one_pull = jax.vjp(
        layer_norm, inputs, attn_gain.astype(jnp.float32), attn_shift.astype(jnp.float32)
    )
    act_one = normed_one.astype(jnp.bfloat16)
    projected = jnp.dot(act_one, w_qkv, preferred_element_type=jnp.float32)
    queries = (projected[..., :model_width] + query_bias.astype(jnp.float32)).astype(jnp.bfloat16)
    keys_local = projected[..., model_width : 2 * model_width].astype(jnp.bfloat16)
    values_local = (projected[..., 2 * model_width :] + value_bias.astype(jnp.float32)).astype(
        jnp.bfloat16
    )
    segment_wire = segment_ids.astype(jnp.bfloat16)
    keys_all, values_all, segment_all = (
        lax.all_gather(keys_local, "pos", axis=1, tiled=True),
        lax.all_gather(values_local, "pos", axis=1, tiled=True),
        lax.all_gather(segment_wire, "pos", axis=1, tiled=True),
    )
    query_class, query_branch = classes(
        local_places, segment_ids, group_sizes, prefix_lens, solution_lens, padding_counts, row_len
    )
    key_class, key_branch = classes(
        all_places,
        segment_all.astype(jnp.int32),
        group_sizes,
        prefix_lens,
        solution_lens,
        padding_counts,
        row_len,
    )
    allowed = visible(query_class, query_branch, local_places, key_class, key_branch, all_places)

    def forward_head(triple):
        query_head, key_head, value_head = triple
        scores = head_scores(query_head, key_head, allowed, score_scale)
        top_head = jnp.max(scores, axis=-1)
        weights = jnp.exp(scores - top_head[..., None])
        total_head = jnp.sum(weights, axis=-1)
        probs_low = (weights / total_head[..., None]).astype(jnp.bfloat16)
        mixed_head = jnp.einsum(
            "rqk,rke->rqe", probs_low, value_head, preferred_element_type=jnp.float32
        )
        return (mixed_head, top_head, total_head)

    queries_heads = heads_first(queries)
    mixed_heads, top, total = lax.map(
        forward_head, (queries_heads, heads_first(keys_all), heads_first(values_all))
    )
    mixed_low = heads_last(mixed_heads).astype(jnp.bfloat16)
    resid = inputs + (
        jnp.dot(mixed_low, w_out, preferred_element_type=jnp.float32) + out_bias.astype(jnp.float32)
    )
    normed_two, norm_two_pull = jax.vjp(
        layer_norm, resid, ffn_gain.astype(jnp.float32), ffn_shift.astype(jnp.float32)
    )
    act_two = normed_two.astype(jnp.bfloat16)
    upper = jnp.dot(act_two, w_up, preferred_element_type=jnp.float32) + up_bias.astype(jnp.float32)
    hidden_full, gelu_pull = jax.vjp(gelu_tanh, upper)
    hidden = hidden_full.astype(jnp.bfloat16)
    layer_out = (
        resid
        + (
            jnp.dot(hidden, w_down, preferred_element_type=jnp.float32)
            + down_bias.astype(jnp.float32)
        )
    ).astype(jnp.bfloat16)
    grad_out = cotangent.astype(jnp.float32)
    grad_w_down = outer_sum(hidden, cotangent)
    grad_down_bias = column_sum(grad_out)
    (grad_upper_full,) = gelu_pull(back_through(cotangent, w_down))
    grad_upper = grad_upper_full.astype(jnp.bfloat16)
    grad_w_up = outer_sum(act_two, grad_upper)
    grad_up_bias = column_sum(grad_upper)
    grad_resid_norm, grad_ffn_gain, grad_ffn_shift = norm_two_pull(back_through(grad_upper, w_up))
    grad_resid = grad_out + grad_resid_norm
    grad_attn = grad_resid.astype(jnp.bfloat16)
    grad_w_out = outer_sum(mixed_low, grad_attn)
    grad_out_bias = column_sum(grad_attn)
    grad_mixed = back_through(grad_attn, w_out).astype(jnp.bfloat16)
    keys_again, values_again = (
        lax.all_gather(keys_local, "pos", axis=1, tiled=True),
        lax.all_gather(values_local, "pos", axis=1, tiled=True),
    )
    grad_mixed_heads = heads_first(grad_mixed)

    def backward_head(items):
        query_head, key_head, value_head, grad_head, top_head, total_head = items
        scores = head_scores(query_head, key_head, allowed, score_scale)
        probs = jnp.exp(scores - top_head[..., None]) / total_head[..., None]
        grad_probs = jnp.einsum(
            "rqe,rke->rqk", grad_head, value_head, preferred_element_type=jnp.float32
        )
        delta_head = jnp.sum(probs * grad_probs, axis=-1)
        grad_scores = (probs * (grad_probs - delta_head[..., None])).astype(jnp.bfloat16)
        query_grad = (
            jnp.einsum("rqk,rke->rqe", grad_scores, key_head, preferred_element_type=jnp.float32)
            * score_scale
        ).astype(jnp.bfloat16)
        key_term = (
            jnp.einsum("rqk,rqe->rke", grad_scores, query_head, preferred_element_type=jnp.float32)
            * score_scale
        )
        value_term = jnp.einsum(
            "rqk,rqe->rke",
            probs.astype(jnp.bfloat16),
            grad_head,
            preferred_element_type=jnp.float32,
        )
        return (query_grad, key_term, value_term, delta_head)

    query_heads_grad, key_heads, value_heads, delta = lax.map(
        backward_head,
        (
            queries_heads,
            heads_first(keys_again),
            heads_first(values_again),
            grad_mixed_heads,
            top,
            total,
        ),
    )
    key_sum, value_sum = (
        lax.psum_scatter(heads_last(key_heads), "pos", scatter_dimension=1, tiled=True),
        lax.psum_scatter(heads_last(value_heads), "pos", scatter_dimension=1, tiled=True),
    )
    grad_queries = heads_last(query_heads_grad)
    grad_keys = key_sum.astype(jnp.bfloat16)
    grad_values = value_sum.astype(jnp.bfloat16)
    grad_project = jnp.concatenate([grad_queries, grad_keys, grad_values], axis=-1)
    grad_w_qkv = outer_sum(act_one, grad_project)
    grad_query_bias = column_sum(grad_queries)
    grad_value_bias = column_sum(grad_values)
    grad_input_norm, grad_attn_gain, grad_attn_shift = norm_one_pull(
        back_through(grad_project, w_qkv)
    )
    tokens_grad = (grad_resid + grad_input_norm).astype(jnp.bfloat16)
    summed = lax.psum(
        (
            grad_attn_gain,
            grad_attn_shift,
            grad_w_qkv,
            grad_query_bias,
            grad_value_bias,
            grad_w_out,
            grad_out_bias,
            grad_ffn_gain,
            grad_ffn_shift,
            grad_w_up,
            grad_up_bias,
            grad_w_down,
            grad_down_bias,
        ),
        ("rows", "pos"),
    )
    return (
        layer_out,
        tokens_grad,
        summed[0],
        summed[1],
        summed[2],
        summed[3],
        summed[4],
        summed[5],
        summed[6],
        summed[7],
        summed[8],
        summed[9],
        summed[10],
        summed[11],
        summed[12],
    )


def solution(mesh):
    in_specs = (
        P("rows", "pos", None),
        P("rows", "pos"),
        P("rows", None),
        P("rows", None),
        P("rows", None, None),
        P("rows"),
        P(),
        P(),
        P(),
        P(),
        P(),
        P(),
        P(),
        P(),
        P(),
        P(),
        P(),
        P(),
        P(),
        P("rows", "pos", None),
    )
    out_specs = (
        P("rows", "pos", None),
        P("rows", "pos", None),
        P(),
        P(),
        P(),
        P(),
        P(),
        P(),
        P(),
        P(),
        P(),
        P(),
        P(),
        P(),
        P(),
    )
    return jax.shard_map(
        per_device, mesh=mesh, in_specs=in_specs, out_specs=out_specs, check_vma=False
    )
```

profile of v0, /device:TPU:0, one launch (start us, length us, event | category | flops | bytes accessed | tf_op | source)
XLA Modules:
  0.0 1607.0 jit_solution(12968616290820048877)
XLA Ops:
  39.0 10.9 all_gather.12
  60.9 38.5 %all-gather.5.cloned.1.call-done = bf16[4,2048,768]{2,1,0:T(8,128)(2,1)} async-done(((bf16[4,256,768]{2,1,0:T(8,128)(2,1)}), bf16[4,2048,768]{2,1,0:T(8,128)(2,1)}) %all-gather.5.cloned.1.call-update) | async-done | bytes 12582928 | tf_op jit(solution)/shard_map/all_gather | solution.py:130
  99.3 16.5 %copy.82 = bf16[4,2048,768]{1,2,0:T(8,128)(2,1)} copy(bf16[4,2048,768]{2,1,0:T(8,128)(2,1)} %all-gather.5.cloned.1.call-done) | data formatting | bytes 25165824 | tf_op jit(solution)/shard_map/all_gather | solution.py:130
  115.8 10.7 copy.89
  126.5 47.4 %all-gather.3.cloned.1.call-done = bf16[4,2048,768]{2,1,0:T(8,128)(2,1)} async-done(((bf16[4,256,768]{2,1,0:T(8,128)(2,1)}), bf16[4,2048,768]{2,1,0:T(8,128)(2,1)}) %all-gather.3.cloned.1.call-update) | async-done | bytes 12582928 | tf_op jit(solution)/shard_map/all_gather | solution.py:129
  173.8 16.0 copy.81
  189.9 10.7 copy.88
  200.6 127.0 %while.30 = (s32[]{:T(128)}, bf16[12,4,256,64]{2,3,0,1:T(8,128)(2,1)}, f32[12,4,256]{2,1,0:T(4,128)}, f32[12,4,256]{2,1,0:T(4,128)}, bf16[12,4,256,64]{2,3,1,0:T...) while((s32[]{:T(128)}, ...), condition=%wide.region_13.14_spmd.clone, body=%wide.region_10.13_spmd.clone.sunk | while | flops 564131840 | bytes 28301456 | solution.py:160
  340.7 17.8 %convert_reduce_fusion = (f32[3072]{0:T(1024)}, bf16[4,256,3072]{2,1,0:T(8,128)(2,1)S(1)}) fusion(bf16[4,256,768]{2,1,0:T(8,128)(2,1)S(1)} %copy-done.12, bf16[3072,768]{1,0:T(8,128)(2,1)} %param.41, f32[4,256,3072]{2,1,0:T(8,128)} %fusion.65, f32[3072]{0:T(1024)S(1)} %copy-done.50), kind=kOutput, calls=%fused_computation.65 | convolution fusion | flops 4916769792 | bytes 25190400 | tf_op jit(solution)/shard_map/rpo,io->rpi/dot_general | solution.py:82
  374.3 422.0 %while.31 = (s32[]{:T(128)}, bf16[12,4,256,64]{2,3,0,1:T(8,128)(2,1)}, f32[12,4,2048,64]{2,3,0,1:T(8,128)}, f32[12,4,2048,64]{2,3,0,1:T(8,128)}, bf16[12,4,256,6...) while((s32[]{:T(128)}, ...), condition=%wide.region_20.21_spmd.clone, body=%wide.region_18.20_spmd.clone.sunk | while | flops 1374288896 | bytes 124245304 | solution.py:225
  483.1 9.8 multiply_reduce_fusion.5
  553.5 9.8 multiply_reduce_fusion.5
  588.7 9.8 multiply_reduce_fusion.5
  624.0 9.8 multiply_reduce_fusion.5
  659.1 9.8 multiply_reduce_fusion.5
  796.4 24.7 %copy.99 = f32[4,2048,768]{2,1,0:T(8,128)} copy(f32[4,2048,768]{1,2,0:T(8,128)} %bitcast.185) | data formatting | bytes 50331648 | tf_op jit(solution)/shard_map/reshape | solution.py:59
  821.2 27.0 %copy.101 = f32[4,2048,768]{2,1,0:T(8,128)} copy(f32[4,2048,768]{1,2,0:T(8,128)} %bitcast.184) | data formatting | bytes 50331648 | tf_op jit(solution)/shard_map/reshape | solution.py:59
  856.8 10.8 convolution_bitcast_fusion.1
  867.7 13.2 convolution_bitcast_fusion
  880.8 96.7 %reduce-scatter.3.cloned.1.call-done = f32[4,256,768]{2,1,0:T(8,128)} async-done(((f32[4,2048,768]{2,1,0:T(8,128)}), f32[4,256,768]{2,1,0:T(8,128)}) %reduce-scatter.3.cloned.1.call-update) | async-done | bytes 3145744 | tf_op jit(solution)/shard_map/reduce_scatter | solution.py:237
  980.8 156.6 %reduce-scatter.5.cloned.1.call-done = f32[4,256,768]{2,1,0:T(8,128)} async-done(((f32[4,2048,768]{2,1,0:T(8,128)}), f32[4,256,768]{2,1,0:T(8,128)}) %reduce-scatter.5.cloned.1.call-update) | async-done | bytes 3145744 | tf_op jit(solution)/shard_map/reduce_scatter | solution.py:238
  1153.1 14.9 add_convert_fusion.1
  1178.6 42.5 %all-reduce = (f32[768]{0:T(1024)}, f32[768]{0:T(1024)}, f32[768]{0:T(1024)}, f32[768]{0:T(1024)}, f32[768]{0:T(1024)}, /*index=5*/f32[768]{0:T(1024)}, f32[768]{0:T(1024)}, f32[3072]{0:T(1024)}, f32[768]{0:T(1024)}) all-reduce(f32[768]{0:T(1024)} %get-tuple-element.258, ...), channel_id=1, replica_groups=mesh['rows'=4,'pos'=8] {'rows','pos'}, use_global_device_ids=true, to_apply=%region_26.27 | all-reduce | flops 9216 | bytes 73728 | tf_op jit(solution)/shard_map/psum | solution.py:251
  1221.1 357.8 %all-reduce.4.cloned.1.call-done = (f32[768,2304]{1,0:T(8,128)}, f32[768,768]{1,0:T(8,128)}, f32[768,3072]{1,0:T(8,128)}, f32[3072,768]{1,0:T(8,128)}) async-done(((f32[768,2304]{1,0:T(8,128)}, f32[768,768]{1,0:T(8,128)}, f32[768,3072]{1,0:T(8,128)}, f32[3072,768]{1,0:T(8,128)}), (f32[768,2304]{1,0:T(8,128)}, f32[768,768]{1,0:T(8,128)}, f32[768,3072]{1,0:T(8,128)}, ...) | async-done | bytes 28311568 | tf_op jit(solution)/shard_map/psum | solution.py:251
  (466 shorter events, 630.0 us)
Async XLA Ops:
  7.2 92.1 %all-gather.5.cloned.1.call-start = ((), (), s32[]{:S(2)}) async-start(), calls=%async_computation.3 | async-start | bytes 14155776 | tf_op jit(solution)/shard_map/all_gather | solution.py:130
  24.4 149.4 %all-gather.3.cloned.1.call-start = ((), (), s32[]{:S(2)}) async-start(), calls=%async_computation.2 | async-start | bytes 14155776 | tf_op jit(solution)/shard_map/all_gather | solution.py:129
  27.7 949.9 %reduce-scatter.3.cloned.1.call-start = ((), (), s32[]{:S(2)}) async-start(), calls=%async_computation.4 | async-start | bytes 28311552 | tf_op jit(solution)/shard_map/reduce_scatter | solution.py:237
  28.7 336.0 %copy-start.24 = (f32[768]{0:T(1024)}, f32[768]{0:T(1024)S(1)}, u32[]{:S(2)}) copy-start(f32[768]{0:T(1024)S(1)} %convert_element_type.132) | copy-start | bytes 9220
  29.4 302.8 %copy-start.26 = (f32[768]{0:T(1024)}, f32[768]{0:T(1024)S(1)}, u32[]{:S(2)}) copy-start(f32[768]{0:T(1024)S(1)} %convert_element_type.133) | copy-start | bytes 9220
  189.9 10.7 copy-start.55
  331.6 33.0 %copy-start.3 = (f32[4,256,768]{2,1,0:T(8,128)}, f32[4,256,768]{2,1,0:T(8,128)S(1)}, u32[]{:S(2)}) copy-start(f32[4,256,768]{2,1,0:T(8,128)S(1)} %get-tuple-element.364) | copy-start | bytes 9437188
  331.7 33.0 %copy-start.28 = (f32[4,256]{1,0:T(4,128)}, f32[4,256]{1,0:T(4,128)S(1)}, u32[]{:S(2)}) copy-start(f32[4,256]{1,0:T(4,128)S(1)} %broadcast_multiply_fusion) | copy-start | bytes 12292
  332.2 32.5 %copy-start.30 = (f32[4,256]{1,0:T(4,128)}, f32[4,256]{1,0:T(4,128)S(1)}, u32[]{:S(2)}) copy-start(f32[4,256]{1,0:T(4,128)S(1)} %fusion.92) | copy-start | bytes 12292
  483.1 9.8 copy-start.1
  553.5 9.8 copy-start.1
  821.1 316.3 %reduce-scatter.5.cloned.1.call-start = ((), (), s32[]{:S(2)}) async-start(), calls=%async_computation.5 | async-start | bytes 28311552 | tf_op jit(solution)/shard_map/reduce_scatter | solution.py:238
  848.2 730.7 %all-reduce.4.cloned.1.call-start = ((), (), s32[]{:S(2)}) async-start(), calls=%async_computation.6 | async-start | bytes 56623104 | tf_op jit(solution)/shard_map/psum | solution.py:251
  856.8 10.8 copy-start.13
  856.8 10.8 copy-start.51
  977.6 163.9 %copy-start.40 = (f32[768]{0:T(1024)S(1)}, f32[768]{0:T(1024)}, u32[]{:S(2)}) copy-start(f32[768]{0:T(1024)} %copy-done.39) | copy-start | bytes 9220
  977.6 163.9 %copy-start.42 = (f32[4,256]{1,0:T(4,128)S(1)}, f32[4,256]{1,0:T(4,128)}, u32[]{:S(2)}) copy-start(f32[4,256]{1,0:T(4,128)} %copy-done.41) | copy-start | bytes 12292
  977.6 163.9 %copy-start.59 = (f32[768]{0:T(1024)S(1)}, f32[768]{0:T(1024)}, u32[]{:S(2)}) copy-start(f32[768]{0:T(1024)} %copy-done.58) | copy-start | bytes 9220
  980.8 160.7 %copy-start.38 = (f32[4,256]{1,0:T(4,128)S(1)}, f32[4,256]{1,0:T(4,128)}, u32[]{:S(2)}) copy-start(f32[4,256]{1,0:T(4,128)} %copy-done.37) | copy-start | bytes 12292
  1153.1 14.9 copy-start.9
  1153.1 14.9 copy-start.17
  1153.1 14.9 copy-start.20
  1153.1 14.9 copy-start.22
  1585.5 10.7 slice-start
  (107 other events, 467.7 us)
Sparse Core Ops, SparseCore 0:
  24.5 74.7 all-gather.4
  101.8 71.9 all-gather.2
  821.2 156.2 reduce-scatter.2
  981.0 156.3 reduce-scatter.4
  1148.9 429.9 all-reduce.3
where the time goes:
time: 1620 us; the launch traced here: 1610 us
  waiting for transfers between devices  697 us (43%)
  matrix products  514 us (32%)
  local copies, waits for them, and re-layouts  167 us (10%)
  other arithmetic  160 us (10%)
  blocking collectives  53.4 us (3%)
    psum x1, waiting for transfers between devices, per_device(): lax.psum((grad_attn_gain, grad_attn_shift, grad_w_qkv, grad_query_bias, g...  358 us
    dot_general x24, matrix products, head_scores(): jnp.einsum('rqe,rke->rqk', query_head, key_head, preferred_element_type=j...  179 us
    reduce_scatter x1, waiting for transfers between devices, per_device(): lax.psum_scatter(heads_last(value_heads), 'pos', scatter_dimension=1, til...  157 us
    convert_element_type x12, other arithmetic, backward_head(): (probs * (grad_probs - delta_head[..., None])).astype(jnp.bfloat16)  102 us
    reduce_scatter x1, waiting for transfers between devices, per_device(): lax.psum_scatter(heads_last(key_heads), 'pos', scatter_dimension=1, tiled...  96.7 us
    dot_general x12, matrix products, backward_head(): jnp.einsum('rqk,rqe->rke', probs.astype(jnp.bfloat16), grad_head, preferr...  69.7 us
    reshape x3, local copies, waits for them, and re-layouts, heads_last(): values.transpose(1, 2, 0, 3)  54.9 us
    dot_general x12, matrix products, backward_head(): jnp.einsum('rqk,rke->rqe', grad_scores, key_head, preferred_element_type=...  54.6 us
  transfers between devices with their start and end apart: 5, of which 5 were waited for; matrix products, arithmetic and copies ran while one was open for 9% of the time, Pallas kernels for 0%

commit v1 on v0

--- a/solution.py
+++ b/solution.py
@@ -8,6 +8,19 @@
 EPS = 1e-05
 NEG = -1e30
 GELU_C = 0.7978845608028654
+
+
+def ring_gather(shard, axis, dim):
+    ways = lax.axis_size(axis)
+    up = [(d, (d + 1) % ways) for d in range(ways)]
+    down = [(d, (d - 1) % ways) for d in range(ways)]
+    earlier, later = ([shard], [shard])
+    for _ in range(ways // 2):
+        earlier.append(lax.ppermute(earlier[-1], axis, up))
+    for _ in range((ways - 1) // 2):
+        later.append(lax.ppermute(later[-1], axis, down))
+    line = jnp.concatenate([*earlier[::-1], *later[1:]], axis=dim)
+    return jnp.roll(line, (lax.axis_index(axis) - ways // 2) * shard.shape[dim], axis=dim)
 
 
 def layer_norm(values, gain, shift):
@@ -127,7 +140,7 @@
     segment_wire = segment_ids.astype(jnp.bfloat16)
     keys_all, values_all, segment_all = (
         lax.all_gather(keys_local, "pos", axis=1, tiled=True),
-        lax.all_gather(values_local, "pos", axis=1, tiled=True),
+        ring_gather(values_local, "pos", 1),
         lax.all_gather(segment_wire, "pos", axis=1, tiled=True),
     )
     query_class, query_branch = classes(

time: 1620 us -> 1760 us (1.086)
  waiting for transfers between devices: 697 us -> 765 us
  blocking collectives: 53.4 us -> 93.9 us
  local copies, waits for them, and re-layouts: 167 us -> 197 us
    ppermute x0 -> x7, waiting for transfers between devices: none -> 154 us  [the longest x4 154 us: ring_gather(): earlier.append(lax.ppermute(earlier[-1], axis, up))]
    all_gather x1, waiting for transfers between devices: 47.4 us -> 0.01 us  [per_device(): lax.all_gather(keys_local, 'pos', axis=1, tiled=True)]
    all_gather x1, blocking collectives: 10.9 us -> 51.3 us  [per_device(): lax.all_gather(segment_wire, 'pos', axis=1, tiled=True)]
    all_gather x1, waiting for transfers between devices: 38.5 us -> 0.01 us  [per_device(): lax.all_gather(values_local, 'pos', axis=1, tiled=True)]
    dynamic_slice x0 -> x2, local copies, waits for them, and re-layouts: none -> 21.2 us  [ring_gather(): jnp.roll(line, (lax.axis_index(axis) - ways // 2) * shard.shape[dim], axi...]
    unnamed x140 -> x146, local copies, waits for them, and re-layouts: 52.6 us -> 62.2 us
  transfers between devices with their start and end apart: 5 -> 12, of which waited for: 5 -> 6; matrix products, arithmetic and copies ran while one was open for 9% -> 20% of each run, Pallas kernels for 0% -> 0%
where the time goes in v1:
time: 1760 us; the launch traced here: 1750 us
  waiting for transfers between devices  765 us (43%)
  matrix products  514 us (29%)
  local copies, waits for them, and re-layouts  197 us (11%)
  other arithmetic  158 us (9%)
  blocking collectives  93.9 us (5%)
    psum x1, waiting for transfers between devices, per_device(): lax.psum((grad_attn_gain, grad_attn_shift, grad_w_qkv, grad_query_bias, g...  358 us
    dot_general x24, matrix products, head_scores(): jnp.einsum('rqe,rke->rqk', query_head, key_head, preferred_element_type=j...  179 us
    reduce_scatter x1, waiting for transfers between devices, per_device(): lax.psum_scatter(heads_last(value_heads), 'pos', scatter_dimension=1, til...  156 us
    ppermute x4, waiting for transfers between devices, ring_gather(): earlier.append(lax.ppermute(earlier[-1], axis, up))  154 us
    convert_element_type x12, other arithmetic, backward_head(): (probs * (grad_probs - delta_head[..., None])).astype(jnp.bfloat16)  102 us
    reduce_scatter x1, waiting for transfers between devices, per_device(): lax.psum_scatter(heads_last(key_heads), 'pos', scatter_dimension=1, tiled...  96.3 us
    dot_general x12, matrix products, backward_head(): jnp.einsum('rqk,rqe->rke', probs.astype(jnp.bfloat16), grad_head, preferr...  69.6 us
    unnamed x146, local copies, waits for them, and re-layouts  62.2 us
  transfers between devices with their start and end apart: 12, of which 6 were waited for; matrix products, arithmetic and copies ran while one was open for 20% of the time, Pallas kernels for 0%

profile of v1, /device:TPU:0, one launch (start us, length us, event | category | flops | bytes accessed | tf_op | source)
XLA Modules:
  0.0 1752.6 jit_solution(18382342704667441326)
XLA Ops:
  28.5 38.1 %collective-permute-done = bf16[4,256,768]{2,1,0:T(8,128)(2,1)} collective-permute-done((bf16[4,256,768]{2,1,0:T(8,128)(2,1)}, bf16[4,256,768]{2,1,0:T(8,128)(2,1)}, u32[]{:S(2)}, u32[]{:S(2)}) %collective-permute-start) | collective-permute-done | bytes 1572896 | tf_op jit(solution)/shard_map/ppermute | solution.py:19
  71.0 66.5 %collective-permute-done.1 = bf16[4,256,768]{2,1,0:T(8,128)(2,1)} collective-permute-done((bf16[4,256,768]{2,1,0:T(8,128)(2,1)}, bf16[4,256,768]{2,1,0:T(8,128)(2,1)}, u32[]{:S(2)}, u32[]{:S(2)}) %collective-permute-start.1) | collective-permute-done | bytes 1572896 | tf_op jit(solution)/shard_map/ppermute | solution.py:19
  143.9 51.3 %all_gather.11 = bf16[4,2048]{1,0:T(4,128)(2,1)S(1)} all-gather(bf16[4,256]{1,0:T(4,128)(2,1)S(1)} %get-tuple-element.361), channel_id=1, replica_groups=mesh['rows'=4,'pos'=8] {'pos'}, dimensions={1}, use_global_device_ids=true | all-gather | bytes 18432 | tf_op jit(solution)/shard_map/all_gather | solution.py:144
  211.2 49.6 %collective-permute-done.3 = bf16[4,256,768]{2,1,0:T(8,128)(2,1)} collective-permute-done((bf16[4,256,768]{2,1,0:T(8,128)(2,1)}, bf16[4,256,768]{2,1,0:T(8,128)(2,1)}, u32[]{:S(2)}, u32[]{:S(2)}) %collective-permute-start.3) | collective-permute-done | bytes 1572896 | tf_op jit(solution)/shard_map/ppermute | solution.py:19
  287.9 15.6 copy.83
  303.5 16.7 copy.82
  320.2 10.7 copy.89
  330.9 127.0 %while.30 = (s32[]{:T(128)}, bf16[12,4,256,64]{2,3,0,1:T(8,128)(2,1)}, f32[12,4,256]{2,1,0:T(4,128)}, f32[12,4,256]{2,1,0:T(4,128)}, bf16[12,4,256,64]{2,3,1,0:T...) while((s32[]{:T(128)}, ...), condition=%wide.region_13.14_spmd.clone, body=%wide.region_10.13_spmd.clone.sunk | while | flops 564131840 | bytes 28301456 | solution.py:173
  471.2 17.8 %convert_reduce_fusion = (f32[3072]{0:T(1024)}, bf16[4,256,3072]{2,1,0:T(8,128)(2,1)S(1)}) fusion(bf16[4,256,768]{2,1,0:T(8,128)(2,1)S(1)} %copy-done.13, bf16[3072,768]{1,0:T(8,128)(2,1)} %param.41, f32[4,256,3072]{2,1,0:T(8,128)} %fusion.65, f32[3072]{0:T(1024)S(1)} %copy-done.46), kind=kOutput, calls=%fused_computation.65 | convolution fusion | flops 4916769792 | bytes 25190400 | tf_op jit(solution)/shard_map/rpo,io->rpi/dot_general | solution.py:95
  504.6 16.7 copy.94
  521.3 421.6 %while.31 = (s32[]{:T(128)}, bf16[12,4,256,64]{2,3,0,1:T(8,128)(2,1)}, f32[12,4,2048,64]{2,3,0,1:T(8,128)}, f32[12,4,2048,64]{2,3,0,1:T(8,128)}, bf16[12,4,256,6...) while((s32[]{:T(128)}, ...), condition=%wide.region_20.21_spmd.clone, body=%wide.region_18.20_spmd.clone.sunk | while | flops 1374288896 | bytes 124245304 | solution.py:238
  629.9 9.8 multiply_reduce_fusion.5
  735.4 9.8 multiply_reduce_fusion.5
  840.9 9.8 multiply_reduce_fusion.5
  911.3 9.8 multiply_reduce_fusion.5
  943.0 24.7 %copy.101 = f32[4,2048,768]{2,1,0:T(8,128)} copy(f32[4,2048,768]{1,2,0:T(8,128)} %bitcast.192) | data formatting | bytes 50331648 | tf_op jit(solution)/shard_map/reshape | solution.py:72
  967.7 26.9 %copy.103 = f32[4,2048,768]{2,1,0:T(8,128)} copy(f32[4,2048,768]{1,2,0:T(8,128)} %bitcast.191) | data formatting | bytes 50331648 | tf_op jit(solution)/shard_map/reshape | solution.py:72
  1003.0 10.8 convolution_bitcast_fusion.1
  1013.8 13.2 convolution_bitcast_fusion
  1027.0 96.3 %reduce-scatter.3.cloned.1.call-done = f32[4,256,768]{2,1,0:T(8,128)} async-done(((f32[4,2048,768]{2,1,0:T(8,128)}), f32[4,256,768]{2,1,0:T(8,128)}) %reduce-scatter.3.cloned.1.call-update) | async-done | bytes 3145744 | tf_op jit(solution)/shard_map/reduce_scatter | solution.py:250
  1126.6 156.5 %reduce-scatter.5.cloned.1.call-done = f32[4,256,768]{2,1,0:T(8,128)} async-done(((f32[4,2048,768]{2,1,0:T(8,128)}), f32[4,256,768]{2,1,0:T(8,128)}) %reduce-scatter.5.cloned.1.call-update) | async-done | bytes 3145744 | tf_op jit(solution)/shard_map/reduce_scatter | solution.py:251
  1298.8 14.9 add_convert_fusion.1
  1324.2 42.5 %all-reduce = (f32[768]{0:T(1024)}, f32[768]{0:T(1024)}, f32[768]{0:T(1024)}, f32[768]{0:T(1024)}, f32[768]{0:T(1024)}, /*index=5*/f32[768]{0:T(1024)}, f32[768]{0:T(1024)}, f32[3072]{0:T(1024)}, f32[768]{0:T(1024)}) all-reduce(f32[768]{0:T(1024)} %get-tuple-element.258, ...), channel_id=1, replica_groups=mesh['rows'=4,'pos'=8] {'rows','pos'}, use_global_device_ids=true, to_apply=%region_26.27 | all-reduce | flops 9216 | bytes 73728 | tf_op jit(solution)/shard_map/psum | solution.py:264
  1366.8 357.8 %all-reduce.4.cloned.1.call-done = (f32[768,2304]{1,0:T(8,128)}, f32[768,768]{1,0:T(8,128)}, f32[768,3072]{1,0:T(8,128)}, f32[3072,768]{1,0:T(8,128)}) async-done(((f32[768,2304]{1,0:T(8,128)}, f32[768,768]{1,0:T(8,128)}, f32[768,3072]{1,0:T(8,128)}, f32[3072,768]{1,0:T(8,128)}), (f32[768,2304]{1,0:T(8,128)}, f32[768,768]{1,0:T(8,128)}, f32[768,3072]{1,0:T(8,128)}, ...) | async-done | bytes 28311568 | tf_op jit(solution)/shard_map/psum | solution.py:264
  (489 shorter events, 671.4 us)
Async XLA Ops:
  7.2 296.3 %all-gather.3.cloned.1.call-start = ((), (), s32[]{:S(2)}) async-start(), calls=%async_computation.2 | async-start | bytes 14155776 | tf_op jit(solution)/shard_map/all_gather | solution.py:142
  22.8 481.8 %all-gather.5.cloned.1.call-start = ((), (), s32[]{:S(2)}) async-start(), calls=%async_computation.3 | async-start | bytes 14155776 | tf_op jit(solution)/shard_map/all_gather | solution.py:209
  22.9 46.5 %copy-start.60 = (s32[4,2]{0,1:T(2,128)S(1)}, s32[4,2]{0,1:T(2,128)}, u32[]{:S(2)}) copy-start(s32[4,2]{0,1:T(2,128)} %param.26) | copy-start | bytes 100
  22.9 46.5 %copy-start.55 = (s32[4,2,16]{2,1,0:T(2,128)S(1)}, s32[4,2,16]{2,1,0:T(2,128)}, u32[]{:S(2)}) copy-start(s32[4,2,16]{2,1,0:T(2,128)} %param.28) | copy-start | bytes 1540
  22.9 114.6 %copy-start.48 = (s32[4,2]{0,1:T(2,128)S(1)}, s32[4,2]{0,1:T(2,128)}, u32[]{:S(2)}) copy-start(s32[4,2]{0,1:T(2,128)} %param.27) | copy-start | bytes 100
  28.0 38.6 %collective-permute-start = (bf16[4,256,768]{2,1,0:T(8,128)(2,1)}, bf16[4,256,768]{2,1,0:T(8,128)(2,1)}, u32[]{:S(2)}, u32[]{:S(2)}) collective-permute-start(bf16[4,256,768]{2,1,0:T(8,128)(2,1)} %get-tuple-element.356), channel_id=1, source_target_pairs={{0,1},{1,2},{2,3},{3,4},{4,5},{5,6},{6,7},{7,0},{8,9},{9,10},{10,1... | collective-permute-start | bytes 4718600 | tf_op jit(solution)/shard_map/ppermute | solution.py:19
  66.6 70.9 %collective-permute-start.1 = (bf16[4,256,768]{2,1,0:T(8,128)(2,1)}, bf16[4,256,768]{2,1,0:T(8,128)(2,1)}, u32[]{:S(2)}, u32[]{:S(2)}) collective-permute-start(bf16[4,256,768]{2,1,0:T(8,128)(2,1)} %collective-permute-done), channel_id=1, source_target_pairs={{0,1},{1,2},{2,3},{3,4},{4,5},{5,6},{6,7},{7,0},{8,9},{9,10},{10,1... | collective-permute-start | bytes 4718600 | tf_op jit(solution)/shard_map/ppermute | solution.py:19
  66.6 73.1 %collective-permute-start.4 = (bf16[4,256,768]{2,1,0:T(8,128)(2,1)}, bf16[4,256,768]{2,1,0:T(8,128)(2,1)}, u32[]{:S(2)}, u32[]{:S(2)}) collective-permute-start(bf16[4,256,768]{2,1,0:T(8,128)(2,1)} %get-tuple-element.356), channel_id=1, source_target_pairs={{0,7},{1,0},{2,1},{3,2},{4,3},{5,4},{6,5},{7,6},{8,15},{9,8},{10,9... | collective-permute-start | bytes 4718600 | tf_op jit(solution)/shard_map/ppermute | solution.py:21
  69.3 1053.9 %reduce-scatter.3.cloned.1.call-start = ((), (), s32[]{:S(2)}) async-start(), calls=%async_computation.4 | async-start | bytes 28311552 | tf_op jit(solution)/shard_map/reduce_scatter | solution.py:250
  137.5 58.6 %collective-permute-start.2 = (bf16[4,256,768]{2,1,0:T(8,128)(2,1)}, bf16[4,256,768]{2,1,0:T(8,128)(2,1)}, u32[]{:S(2)}, u32[]{:S(2)}) collective-permute-start(bf16[4,256,768]{2,1,0:T(8,128)(2,1)} %collective-permute-done.1), channel_id=1, source_target_pairs={{0,1},{1,2},{2,3},{3,4},{4,5},{5,6},{6,7},{7,0},{8,9},{9,10},{10,1... | collective-permute-start | bytes 4718600 | tf_op jit(solution)/shard_map/ppermute | solution.py:19
  139.0 56.3 %copy-start.50 = (s32[256]{0:T(256)}, s32[256]{0:T(256)S(1)}, u32[]{:S(2)}) copy-start(s32[256]{0:T(256)S(1)} %iota_add_fusion) | copy-start | bytes 3076
  139.7 57.9 %collective-permute-start.5 = (bf16[4,256,768]{2,1,0:T(8,128)(2,1)}, bf16[4,256,768]{2,1,0:T(8,128)(2,1)}, u32[]{:S(2)}, u32[]{:S(2)}) collective-permute-start(bf16[4,256,768]{2,1,0:T(8,128)(2,1)} %collective-permute-done.4), channel_id=1, source_target_pairs={{0,7},{1,0},{2,1},{3,2},{4,3},{5,4},{6,5},{7,6},{8,15},{9,8},{10,9... | collective-permute-start | bytes 4718600 | tf_op jit(solution)/shard_map/ppermute | solution.py:21
  196.1 64.6 %collective-permute-start.3 = (bf16[4,256,768]{2,1,0:T(8,128)(2,1)}, bf16[4,256,768]{2,1,0:T(8,128)(2,1)}, u32[]{:S(2)}, u32[]{:S(2)}) collective-permute-start(bf16[4,256,768]{2,1,0:T(8,128)(2,1)} %collective-permute-done.2), channel_id=1, source_target_pairs={{0,1},{1,2},{2,3},{3,4},{4,5},{5,6},{6,7},{7,0},{8,9},{9,10},{10,1... | collective-permute-start | bytes 4718600 | tf_op jit(solution)/shard_map/ppermute | solution.py:19
  197.6 72.5 %collective-permute-start.6 = (bf16[4,256,768]{2,1,0:T(8,128)(2,1)}, bf16[4,256,768]{2,1,0:T(8,128)(2,1)}, u32[]{:S(2)}, u32[]{:S(2)}) collective-permute-start(bf16[4,256,768]{2,1,0:T(8,128)(2,1)} %collective-permute-done.5), channel_id=1, source_target_pairs={{0,7},{1,0},{2,1},{3,2},{4,3},{5,4},{6,5},{7,6},{8,15},{9,8},{10,9... | collective-permute-start | bytes 4718600 | tf_op jit(solution)/shard_map/ppermute | solution.py:21
  201.4 293.7 %copy-start.25 = (f32[768]{0:T(1024)}, f32[768]{0:T(1024)S(1)}, u32[]{:S(2)}) copy-start(f32[768]{0:T(1024)S(1)} %convert_element_type.132) | copy-start | bytes 9220
  202.1 260.4 %copy-start.27 = (f32[768]{0:T(1024)}, f32[768]{0:T(1024)S(1)}, u32[]{:S(2)}) copy-start(f32[768]{0:T(1024)S(1)} %convert_element_type.133) | copy-start | bytes 9220
  462.0 33.1 %copy-start.3 = (f32[4,256,768]{2,1,0:T(8,128)}, f32[4,256,768]{2,1,0:T(8,128)S(1)}, u32[]{:S(2)}) copy-start(f32[4,256,768]{2,1,0:T(8,128)S(1)} %get-tuple-element.364) | copy-start | bytes 9437188
  462.1 33.1 %copy-start.29 = (f32[4,256]{1,0:T(4,128)}, f32[4,256]{1,0:T(4,128)S(1)}, u32[]{:S(2)}) copy-start(f32[4,256]{1,0:T(4,128)S(1)} %broadcast_multiply_fusion) | copy-start | bytes 12292
  967.7 315.4 %reduce-scatter.5.cloned.1.call-start = ((), (), s32[]{:S(2)}) async-start(), calls=%async_computation.5 | async-start | bytes 28311552 | tf_op jit(solution)/shard_map/reduce_scatter | solution.py:251
  994.7 729.8 %all-reduce.4.cloned.1.call-start = ((), (), s32[]{:S(2)}) async-start(), calls=%async_computation.6 | async-start | bytes 56623104 | tf_op jit(solution)/shard_map/psum | solution.py:264
  1123.2 163.9 %copy-start.36 = (f32[768]{0:T(1024)S(1)}, f32[768]{0:T(1024)}, u32[]{:S(2)}) copy-start(f32[768]{0:T(1024)} %copy-done.35) | copy-start | bytes 9220
  1123.2 163.9 %copy-start.38 = (f32[4,256]{1,0:T(4,128)S(1)}, f32[4,256]{1,0:T(4,128)}, u32[]{:S(2)}) copy-start(f32[4,256]{1,0:T(4,128)} %copy-done.37) | copy-start | bytes 12292
  1123.2 163.9 %copy-start.54 = (f32[768]{0:T(1024)S(1)}, f32[768]{0:T(1024)}, u32[]{:S(2)}) copy-start(f32[768]{0:T(1024)} %copy-done.53) | copy-start | bytes 9220
  1126.6 160.6 %copy-start.34 = (f32[4,256]{1,0:T(4,128)S(1)}, f32[4,256]{1,0:T(4,128)}, u32[]{:S(2)}) copy-start(f32[4,256]{1,0:T(4,128)} %copy-done.33) | copy-start | bytes 12292
  (110 other events, 628.6 us)
Sparse Core Ops, SparseCore 0:
  22.9 114.5 all-gather.2
  140.0 114.3 all-gather.4
  967.8 155.3 reduce-scatter.2
  1126.7 156.3 reduce-scatter.4
  1294.5 429.9 all-reduce.3
